TPU v7x, 256 devices: a whole 4x4x8 slice. The times are simulated.
256 devices in a mesh: ctx: 64 (over z, x, core), head: 4 (over y).
Axes of the slice: x: 4, y: 4, z: 8, core: 2. Of those that a mesh axis runs over, the one named last changes fastest.
Arguments:
- queries: bfloat16 [8192, 6144], P('ctx', 'head'), may hold values from -0.75 to 0.75
- keys: bfloat16 [8192, 6144], P('ctx', 'head'), may hold values from -0.75 to 0.75
- values: bfloat16 [8192, 6144], P('ctx', 'head'), may hold values from -1.2 to 1.2
- normed_grad: bfloat16 [8192, 6144], P('ctx', 'head'), may hold values from -1.5 to 1.5
- gain: bfloat16 [6144], P('head'), may hold values from 0.5 to 1.5
- segment: int32 [8192], P('ctx'), may hold values from 0 to 15, never falling along the last dimension, each value on 1 to 2048 neighbouring positions
- plan: int32 [8192], replicated, may hold values from 0 to 8191, as said below
Outputs:
- normed: bfloat16 [8192, 6144], P('ctx', 'head')
- query_grad: bfloat16 [8192, 6144], P('ctx', 'head')
- key_grad: bfloat16 [8192, 6144], P('ctx', 'head')
- value_grad: bfloat16 [8192, 6144], P('ctx', 'head')
Inputs may be any that keep to these rules, and one draw needn't show every extreme that they name: `plan`: A permutation. Loader rows come in aligned blocks of 2 rows that stay together and in order, and the rows held by one index of ctx send exactly one such block to each index of ctx.
All inputs are finite; a program needn't handle non-finite values.
Results may differ from a plain program's by a relative error of at most 0.012.
Values may be sent and summed in bfloat16 or wider, within the bound.
A program may use at most 128 MiB of HBM per device.

v0:
```python
import jax
import jax.numpy as jnp
from jax import lax
from jax.sharding import PartitionSpec as P

HEADS = 48
HEAD_DIM = 128


def entering(value, axis, join, neutral, backward):
    count = lax.axis_size(axis)
    place = lax.axis_index(axis)
    ahead = count - 1 - place if backward else place
    gathered = jax.tree.map(
        lambda a, kind: lax.all_gather(a.astype(kind), axis),
        value,
        (jnp.bfloat16, jnp.bfloat16, jnp.bfloat16),
    )
    state = jax.tree.map(lambda a, e: jnp.zeros_like(a) + jnp.asarray(e, a.dtype), value, neutral)

    def one(lap, state):
        source = count - 1 - lap if backward else lap
        return join(
            state,
            jax.tree.map(
                lambda a, own: lax.dynamic_index_in_dim(a, source, 0, False).astype(own.dtype),
                gathered,
                value,
            ),
        )

    return lax.fori_loop(0, ahead, one, state)


def pick_joined(empty_first, empty_second, first_part, second_part, joined):
    return tuple(
        (
            jnp.where(empty_first, second_leaf, jnp.where(empty_second, first_leaf, joined_leaf))
            for first_leaf, second_leaf, joined_leaf in zip(first_part, second_part, joined)
        )
    )


def join_forward(lower_part, upper_part):
    carries = ((lower_part[1] == upper_part[0]) & (upper_part[0] == upper_part[1])).astype(
        jnp.float32
    )
    joined = (lower_part[0], upper_part[1], upper_part[2] + carries * lower_part[2])
    return pick_joined(lower_part[0] < -0.5, upper_part[0] < -0.5, lower_part, upper_part, joined)


def join_backward(higher, lower_part):
    carries = ((lower_part[1] == higher[0]) & (lower_part[0] == lower_part[1])).astype(jnp.float32)
    joined = (lower_part[0], higher[1], lower_part[2] + carries * higher[2])
    return pick_joined(higher[0] < -0.5, lower_part[0] < -0.5, higher, lower_part, joined)


def empty_element(like_state):
    return (
        jnp.full((1,), -1.0, jnp.float32),
        jnp.full((1,), -1.0, jnp.float32),
        jnp.zeros_like(like_state),
    )


def forward_carry(key_seq, value_seq, seg_f):
    tail_rows = (seg_f == seg_f[-1])[:, None, None]
    local_state = jnp.einsum(
        "ihd,ihe->hde",
        jnp.where(tail_rows, key_seq, jnp.zeros_like(key_seq)),
        value_seq,
        preferred_element_type=jnp.float32,
    )
    return entering(
        (seg_f[:1], seg_f[-1:], local_state), "ctx", join_forward, empty_element(local_state), False
    )


def shards(queries, keys, values, normed_grad, gain, segment, plan):
    row_count, row_width = queries.shape
    heads_here = row_width // HEAD_DIM
    total_width = HEADS * HEAD_DIM
    ctx_size = lax.axis_size("ctx")
    unit_rows = row_count // ctx_size
    own_index = lax.axis_index("ctx")
    starts = plan.reshape(ctx_size, ctx_size, unit_rows)[:, :, 0] // unit_rows
    targets = starts // ctx_size
    places = starts % ctx_size
    columns = jnp.arange(ctx_size, dtype=jnp.int32)
    own_targets = lax.dynamic_index_in_dim(targets, own_index, 0, keepdims=False)
    chosen = jnp.sum(
        jnp.where(own_targets[None, :] == columns[:, None], columns[None, :], 0), axis=1
    )
    arrival = jnp.sum(jnp.where(targets == own_index, places, 0), axis=1)
    settle_order = jnp.sum(
        jnp.where(arrival[None, :] == columns[:, None], columns[None, :], 0), axis=1
    )

    def outgoing(source_rows):
        return jnp.take(source_rows.reshape(ctx_size, unit_rows, row_width), chosen, axis=0)

    def seq_rows(block_set):
        return block_set.reshape(row_count, heads_here, HEAD_DIM)

    seg_f = segment.astype(jnp.float32)
    received = (
        lax.all_to_all(outgoing(queries), "ctx", split_axis=0, concat_axis=0, tiled=True),
        lax.all_to_all(outgoing(keys), "ctx", split_axis=0, concat_axis=0, tiled=True),
        lax.all_to_all(outgoing(values), "ctx", split_axis=0, concat_axis=0, tiled=True),
    )
    query_block, key_block, value_block = tuple(
        (jnp.take(block_set, settle_order, axis=0) for block_set in received)
    )
    query_seq = seq_rows(query_block)
    key_seq = seq_rows(key_block)
    value_seq = seq_rows(value_block)
    prefix = forward_carry(key_seq, value_seq, seg_f)
    positions = jnp.arange(row_count, dtype=jnp.int32)
    visible = (positions[:, None] >= positions[None, :]) & (segment[:, None] == segment[None, :])
    scores = jnp.einsum("ihd,jhd->hij", query_seq, key_seq, preferred_element_type=jnp.float32)
    weights_b = jnp.where(visible[None], scores, 0.0).astype(jnp.bfloat16)
    carried_in = prefix[2].astype(jnp.bfloat16)
    resume = (seg_f == prefix[1][0]).astype(jnp.float32)[:, None, None]
    attended = jnp.einsum("hij,jhe->ihe", weights_b, value_seq, preferred_element_type=jnp.float32)
    attended = attended + resume * jnp.einsum(
        "ihd,hde->ihe", query_seq, carried_in, preferred_element_type=jnp.float32
    )
    attn_f = attended.astype(jnp.bfloat16).reshape(row_count, row_width).astype(jnp.float32)
    gain_f = gain.astype(jnp.float32)
    scaled_grad = normed_grad.astype(jnp.float32) * gain_f
    squares = lax.psum(jnp.sum(attn_f * attn_f, axis=1), "head")
    inverse = lax.rsqrt(squares / total_width + 1e-05)
    normal_part = attn_f * inverse[:, None]
    projection = lax.psum(jnp.sum(scaled_grad * normal_part, axis=1), "head") / total_width
    normed = (normal_part * gain_f).astype(jnp.bfloat16)
    attn_grad = (inverse[:, None] * (scaled_grad - normal_part * projection[:, None])).astype(
        jnp.bfloat16
    )
    grad_seq = attn_grad.reshape(row_count, heads_here, HEAD_DIM)
    head_rows = (seg_f == seg_f[0])[:, None, None]
    head_state = jnp.einsum(
        "ihd,ihe->hde",
        jnp.where(head_rows, query_seq, jnp.zeros_like(query_seq)),
        grad_seq,
        preferred_element_type=jnp.float32,
    )
    suffix = entering(
        (seg_f[:1], seg_f[-1:], head_state), "ctx", join_backward, empty_element(head_state), True
    )
    carried_back = suffix[2].astype(jnp.bfloat16)
    reaches = (seg_f == suffix[0][0]).astype(jnp.float32)[:, None, None]
    grad_scores = jnp.einsum(
        "ihe,jhe->hij", grad_seq, value_seq, preferred_element_type=jnp.float32
    )
    grad_weights = jnp.where(visible[None], grad_scores, 0.0).astype(jnp.bfloat16)
    query_grad = jnp.einsum(
        "hij,jhd->ihd", grad_weights, key_seq, preferred_element_type=jnp.float32
    )
    query_grad = query_grad + resume * jnp.einsum(
        "ihe,hde->ihd", grad_seq, carried_in, preferred_element_type=jnp.float32
    )
    key_grad = jnp.einsum(
        "hij,ihd->jhd", grad_weights, query_seq, preferred_element_type=jnp.float32
    )
    key_grad = key_grad + reaches * jnp.einsum(
        "jhe,hde->jhd", value_seq, carried_back, preferred_element_type=jnp.float32
    )
    value_grad = jnp.einsum("hij,ihe->jhe", weights_b, grad_seq, preferred_element_type=jnp.float32)
    value_grad = value_grad + reaches * jnp.einsum(
        "jhd,hde->jhe", key_seq, carried_back, preferred_element_type=jnp.float32
    )
    return (
        normed,
        query_grad.astype(jnp.bfloat16).reshape(row_count, row_width),
        key_grad.astype(jnp.bfloat16).reshape(row_count, row_width),
        value_grad.astype(jnp.bfloat16).reshape(row_count, row_width),
    )


def solution(mesh):
    placed = (
        P("ctx", "head"),
        P("ctx", "head"),
        P("ctx", "head"),
        P("ctx", "head"),
        P("head"),
        P("ctx"),
        P(),
    )
    return jax.shard_map(
        shards,
        mesh=mesh,
        in_specs=placed,
        out_specs=(P("ctx", "head"), P("ctx", "head"), P("ctx", "head"), P("ctx", "head")),
        check_vma=False,
    )
```

profile of v0, /device:TPU:1, one launch (start us, length us, event | category | flops | bytes accessed | tf_op | source)
XLA Modules:
  0.0 1144.5 jit_solution(1512498876750266373)
XLA Ops:
  7.2 2.8 reshape.122
  19.1 2.1 broadcast_select_fusion.5
  21.2 27.9 %all_to_all.15 = bf16[64,2,1536]{2,1,0:T(2,128)(2,1)S(1)} all-to-all(bf16[64,2,1536]{2,1,0:T(2,128)(2,1)S(1)} %get-tuple-element.229), channel_id=1, replica_groups=mesh['ctx'=64,'head'=4] {'ctx'}, dimensions={0} | all-to-all | bytes 786432 | tf_op jit(solution)/shard_map/all_to_all | solution.py:109
  49.1 5.4 all-to-all-start.1
  54.7 15.1 %all-to-all-done.1 = bf16[64,2,1536]{2,1,0:T(2,128)(2,1)S(1)} async-done(((bf16[64,2,1536]{2,1,0:T(2,128)(2,1)}), bf16[64,2,1536]{2,1,0:T(2,128)(2,1)S(1)}, u32[]{:S(2)}, u32[]{:S(2)}) %all-to-all-start.1) | async-done | bytes 393248 | tf_op jit(solution)/shard_map/all_to_all | solution.py:107
  69.7 5.4 all-to-all-start.2
  76.7 2.0 broadcast_compare_fusion
  81.4 9.0 all-to-all-done.2
  101.3 126.5 %all-reduce.2 = (bf16[64]{0:T(256)(128)(2,1)S(1)}, bf16[64]{0:T(256)(128)(2,1)S(1)}) all-reduce(bf16[64]{0:T(256)(128)(2,1)S(1)} %dynamic-update-slice, bf16[64]{0:T(256)(128)(2,1)S(1)} %dynamic-update-slice.1), channel_id=2, replica_groups=mesh['ctx'=64,'head'=4] {'ctx'}, use_global_device_ids=true, to_apply=%add | all-reduce | flops 128 | bytes 512
  231.6 6.2 while.30
  239.6 8.7 psum.14
  248.5 6.0 psum.15
  255.7 2.3 convolution_convert_fusion
  257.9 1.9 copy.88
  261.9 494.0 %all-gather.9.cloned.1.call-done = bf16[768,128,128]{2,1,0:T(8,128)(2,1)} async-done(((bf16[12,128,128]{2,1,0:T(8,128)(2,1)}), bf16[768,128,128]{2,1,0:T(8,128)(2,1)}) %all-gather.9.cloned.1.call-update) | async-done | bytes 25165840 | tf_op jit(solution)/shard_map/all_gather | solution.py:15
  756.0 377.4 %while.31 = (s32[]{:T(128)}, f32[1]{0:T(128)}, f32[12,128,128]{2,1,0:T(8,128)S(1)}, s32[]{:T(128)}, bf16[64,1]{0,1:T(2,128)(2,1)S(1)}, /*index=5*/bf16[64,12,128...) while((s32[]{:T(128)}, f32[1]{0:T(128)}, ...), condition=%wide.region_10.12_spmd, body=%wide.region_9.11_spmd.sunk | while | flops 983054 | bytes 1966339 | solution.py:32
  790.9 1.6 convert_select_fusion.5
  797.0 1.6 convert_select_fusion.5
  851.8 1.6 convert_select_fusion.5
  906.6 1.6 convert_select_fusion.5
  912.7 1.6 convert_select_fusion.5
  967.5 1.6 convert_select_fusion.5
  1022.2 1.6 convert_select_fusion.5
  1028.3 1.6 convert_select_fusion.5
  (189 shorter events, 164.0 us)
Async XLA Ops:
  7.2 230.7 %copy-start.2 = (s32[128]{0:T(128)S(1)}, s32[128]{0:T(128)}, u32[]{:S(2)}) copy-start(s32[128]{0:T(128)} %param.18) | copy-start | bytes 1540
  49.1 20.6 %all-to-all-start.1 = ((bf16[64,2,1536]{2,1,0:T(2,128)(2,1)}), bf16[64,2,1536]{2,1,0:T(2,128)(2,1)S(1)}, u32[]{:S(2)}, u32[]{:S(2)}) async-start(bf16[64,2,1536]{2,1,0:T(2,128)(2,1)} %get-tuple-element.230), calls=%async_computation.1 | async-start | bytes 786432 | tf_op jit(solution)/shard_map/all_to_all | solution.py:107
  69.7 20.6 %all-to-all-start.2 = ((bf16[64,2,1536]{2,1,0:T(2,128)(2,1)}), bf16[64,2,1536]{2,1,0:T(2,128)(2,1)S(1)}, u32[]{:S(2)}, u32[]{:S(2)}) async-start(bf16[64,2,1536]{2,1,0:T(2,128)(2,1)} %get-tuple-element.231), calls=%async_computation.2 | async-start | bytes 786432 | tf_op jit(solution)/shard_map/all_to_all | solution.py:108
  75.2 156.3 %all-gather.7.cloned.1.call-start = ((), (), s32[]{:S(2)}) async-start(), calls=%async_computation.3 | async-start | bytes 25559040 | tf_op jit(solution)/shard_map/all_gather | solution.py:15
  94.8 661.1 %all-gather.9.cloned.1.call-start = ((), (), s32[]{:S(2)}) async-start(), calls=%async_computation.4 | async-start | bytes 25559040 | tf_op jit(solution)/shard_map/all_gather | solution.py:15
  229.3 8.6 copy-start
  255.7 880.8 %copy-start.1 = (bf16[12,128,128]{2,1,0:T(8,128)(2,1)S(1)}, bf16[12,128,128]{2,1,0:T(8,128)(2,1)}, u32[]{:S(2)}) copy-start(bf16[12,128,128]{2,1,0:T(8,128)(2,1)} %fusion.2) | copy-start | bytes 1179652
Sparse Core Ops, SparseCore 0:
  95.0 117.6 all-gather.6
  258.1 497.8 all-gather.8
where the time goes:
time: 1160 us; the launch traced here: 1140 us
  waiting for transfers between devices  518 us (45%)
  loops' own time  244 us (21%)
  blocking collectives  169 us (15%)
  other arithmetic  111 us (10%)
  local copies, waits for them, and re-layouts  66.8 us (6%)
  between operations  14.3 us (1%)
    all_gather x2, waiting for transfers between devices, entering(): lax.all_gather(a.astype(kind), axis)  494 us
    another operation x2, loops' own time, entering(): return lax.fori_loop(0, ahead, one, state)  244 us
    unnamed x1, blocking collectives  126 us
    select_n x63, other arithmetic, pick_joined(): jnp.where(empty_first, second_leaf, jnp.where(empty_second, first_leaf, j...  101 us
    dynamic_slice x63, local copies, waits for them, and re-layouts, one(): lax.dynamic_index_in_dim(a, source, 0, False).astype(own.dtype)  38.8 us
    all_to_all x1, blocking collectives, shards(): lax.all_to_all(outgoing(values), 'ctx', split_axis=0, concat_axis=0, tile...  27.9 us
  transfers between devices with their start and end apart: 4, of which 3 were waited for; matrix products, arithmetic and copies ran while one was open for 2% of the time, Pallas kernels for 0%

commit v1 on v0

v1 whole, which is shorter than its diff:
```python
import jax
import jax.numpy as jnp
from jax import lax
from jax.experimental import pallas as pl
from jax.experimental.pallas import tpu as pltpu
from jax.sharding import PartitionSpec as P

HEADS = 48
HEAD_DIM = 128
ROWS = 128
LINES = 8
GROUP = 8
OWN_HEADS = 12
CHUNKS = 3
CHUNK_HEADS = OWN_HEADS // CHUNKS
WIDE = CHUNK_HEADS * HEAD_DIM
PARCELS = 3 * CHUNKS
BAND = ROWS // LINES
SLICE = WIDE // GROUP
HEAD_PEERS = 4
MESH = pl.DeviceIdType.MESH
F32 = jnp.float32
BF16 = jnp.bfloat16
Z_ORDER = (4, 3, 5, 2, 6, 1, 7)
G_ORDER = (4, 3, 5, 2, 6, 1, 7)


def nn(a, b):
    return lax.dot_general(a, b, (((1,), (0,)), ((), ())), preferred_element_type=F32)


def nt(a, b):
    return lax.dot_general(a, b, (((1,), (1,)), ((), ())), preferred_element_type=F32)


def tn(a, b):
    return lax.dot_general(a, b, (((0,), (0,)), ((), ())), preferred_element_type=F32)


def iota(dim):
    return lax.broadcasted_iota(jnp.int32, (ROWS, ROWS), dim)


def kernel(
    q_hbm, k_hbm, v_hbm, ng_hbm, gain_hbm, seg_hbm, plan_hbm,
    normed_hbm, qg_hbm, kg_hbm, vg_hbm,
    x, a, b, c, d, seq, ng, gain, seg, plan,
    seg_line, seg_all, mid, settle, vis, vist, tails, heads, resume, reaches,
    sf, srf, rf, zrf, csf, crf, sb, srb, rb, zrb, csb, crb,
    att, gr, wt, gwt, sq_send, sq_recv, kg_part, vg_part, o_n, o_q, o_k, o_v,
    load_sem, out_sem, seg_sem, send_sem, recv_sem,
):
    me = lax.axis_index("ctx")
    y = lax.axis_index("head")
    z = lax.div(me, GROUP)
    g = lax.rem(me, GROUP)

    def z_peer(dz):
        return lax.rem(z + dz, LINES)

    def g_peer(dg):
        return lax.rem(g + dg, GROUP)

    def ctx_of(zz, gg):
        return zz * GROUP + gg

    def band(i):
        return pl.ds(pl.multiple_of(i * BAND, BAND), BAND)

    def send(src, dst, stage, slot, ctx_to, head_to):
        pltpu.make_async_remote_copy(
            src_ref=src, dst_ref=dst, send_sem=send_sem.at[stage], recv_sem=recv_sem.at[slot],
            device_id=(ctx_to, head_to), device_id_type=MESH,
        ).start()

    def took(ref, slot):
        pltpu.make_async_copy(ref, ref, recv_sem.at[slot]).wait()

    order = []
    for j in range(CHUNKS):
        order.append((k_hbm, j))
        order.append((v_hbm, j))
    for j in range(CHUNKS):
        order.append((q_hbm, j))
    small = [
        pltpu.make_async_copy(plan_hbm, plan, load_sem.at[PARCELS]),
        pltpu.make_async_copy(seg_hbm, seg, load_sem.at[PARCELS + 1]),
        pltpu.make_async_copy(gain_hbm, gain, load_sem.at[PARCELS + 2]),
    ]
    for copy in small:
        copy.start()
    loads = []
    for p, (ref, j) in enumerate(order):
        copy = pltpu.make_async_copy(ref.at[:, WIDE * j : WIDE * (j + 1)], x.at[p], load_sem.at[p])
        copy.start()
        loads.append(copy)
    ng_copy = pltpu.make_async_copy(ng_hbm, ng, load_sem.at[PARCELS + 3])
    ng_copy.start()

    barrier = pltpu.get_barrier_semaphore()
    for dz in Z_ORDER:
        pl.semaphore_signal(barrier, inc=1, device_id=(ctx_of(z_peer(dz), g), y), device_id_type=MESH)
    for dg in G_ORDER:
        pl.semaphore_signal(barrier, inc=1, device_id=(ctx_of(z, g_peer(dg)), y), device_id_type=MESH)
    for dy in range(1, HEAD_PEERS):
        pl.semaphore_signal(
            barrier, inc=1, device_id=(me, lax.rem(y + dy, HEAD_PEERS)), device_id_type=MESH
        )

    for copy in small:
        copy.wait()
    rows_i = iota(0)
    cols_i = iota(1)
    own_plan = plan[pl.ds(me, 1), :]
    slot_of = 2 * lax.shift_right_logical(own_plan, 7) + (cols_i[0:1, :] & 1)
    leave = (rows_i == slot_of).astype(F32).astype(BF16)
    for p in range(PARCELS):
        loads[p].wait()
        a[p] = nn(leave, x[p]).astype(BF16)

    seg_row = seg[...]
    seg_f = seg_row.astype(F32)
    seg_lanes = jnp.broadcast_to(seg_f, (ROWS, ROWS))
    seg_rows = seg_lanes.T
    last_here = jnp.broadcast_to(seg_f[:, ROWS - 1 : ROWS], (1, ROWS))
    first_here = jnp.broadcast_to(seg_f[:, 0:1], (1, ROWS))
    same = seg_lanes == seg_rows
    vis[...] = jnp.where(same & (rows_i >= cols_i), 1.0, 0.0)
    vist[...] = jnp.where(same & (cols_i >= rows_i), 1.0, 0.0)
    tails[...] = jnp.where(seg_rows == last_here, 1.0, 0.0).astype(BF16)
    heads[...] = jnp.where(seg_rows == first_here, 1.0, 0.0).astype(BF16)
    seg_line[z, 0:1, :] = last_here
    seg_line[z, 1:2, :] = first_here

    pl.semaphore_wait(barrier, LINES - 1 + GROUP - 1 + HEAD_PEERS - 1)

    for dz in Z_ORDER:
        send(seg_line.at[z], seg_line.at[z], 0, 0, ctx_of(z_peer(dz), g), y)
    for p in range(PARCELS):
        for dz in Z_ORDER:
            zt = z_peer(dz)
            send(a.at[p, band(zt)], b.at[p, band(z)], 1, 2 + p, ctx_of(zt, g), y)
        b[p, band(z), :] = a[p, band(z), :]

    source = ((rows_i & 15) >> 1) * BAND + (rows_i >> 4) * 2 + (rows_i & 1)
    mid[...] = (cols_i == source).astype(F32).astype(BF16)
    plan_all = plan[...]
    lanes = lax.broadcasted_iota(jnp.int32, (LINES * GROUP, ROWS), 1)
    mine = (lax.shift_right_logical(plan_all, 7) == me) & ((lanes & 1) == 0)
    start = jnp.sum(jnp.where(mine, (plan_all & 127).astype(F32), 0.0), axis=1, keepdims=True)
    start = jnp.broadcast_to(start, (LINES * GROUP, ROWS)).astype(BF16)
    pick_rows = lax.broadcasted_iota(jnp.int32, (ROWS, LINES * GROUP), 0)
    pick_cols = lax.broadcasted_iota(jnp.int32, (ROWS, LINES * GROUP), 1)
    pick = (pick_cols == ((pick_rows & 15) >> 1) * GROUP + (pick_rows >> 4)).astype(F32).astype(BF16)
    place = nn(pick, start) + (rows_i & 1).astype(F32)
    settle[...] = jnp.where(cols_i.astype(F32) == place, 1.0, 0.0).T.astype(BF16)

    def first_hop(p):
        took(b.at[p, 0 : ROWS - BAND], 2 + p)
        c[p] = nn(mid[...], b[p]).astype(BF16)
        for dg in G_ORDER:
            gt = g_peer(dg)
            send(c.at[p, band(gt)], d.at[p, band(g)], 2, 2 + PARCELS + p, ctx_of(z, gt), y)
        d[p, band(g), :] = c[p, band(g), :]

    def second_hop(p):
        took(d.at[p, 0 : ROWS - BAND], 2 + PARCELS + p)
        seq[p] = nn(settle[...], d[p]).astype(BF16)

    def lanes_of(hh):
        return slice(HEAD_DIM * hh, HEAD_DIM * (hh + 1))

    def k_of(j, hh):
        return seq[2 * j, :, lanes_of(hh)]

    def v_of(j, hh):
        return seq[2 * j + 1, :, lanes_of(hh)]

    def q_of(j, hh):
        return seq[2 * CHUNKS + j, :, lanes_of(hh)]

    state_slot = 2 + 2 * PARCELS

    def spread(j, local, landed, stage, slot):
        for dg in G_ORDER:
            gt = g_peer(dg)
            send(local.at[j, gt], landed.at[j, g], stage, slot, ctx_of(z, gt), y)
        landed[j, g] = local[j, g]

    def forward_state(j):
        for hh in range(CHUNK_HEADS):
            state = tn(k_of(j, hh) * tails[...], v_of(j, hh)).astype(BF16)
            sf[j, 2 * hh : 2 * hh + 2] = state.reshape(2, SLICE, HEAD_DIM)
        spread(j, sf, srf, 3, state_slot + j)

    def backward_state(j):
        for hh in range(CHUNK_HEADS):
            state = tn(q_of(j, hh) * heads[...], gr[j, :, lanes_of(hh)]).astype(BF16)
            sb[j, 2 * hh : 2 * hh + 2] = state.reshape(2, SLICE, HEAD_DIM)
        spread(j, sb, srb, 6, state_slot + 3 * CHUNKS + j)

    def last_of(zz, gg):
        return seg_all[gg, zz, 0:1, :]

    def first_of(zz, gg):
        return seg_all[gg, zz, 1:2, :]

    def flag(one, two):
        return jnp.where(one == two, 1.0, 0.0)

    def forward_flags():
        z1 = jnp.maximum(z - 1, 0)
        z2 = jnp.maximum(z - 2, 0)
        edge = last_of(z1, GROUP - 1)
        links = [flag(last_of(z, 0), edge)]
        for i in range(1, GROUP):
            links.append(flag(last_of(z, i), last_of(z, i - 1)))
        from_one = jnp.where(z >= 1, 1.0, 0.0)
        from_two = jnp.where(z >= 2, 1.0, 0.0) * flag(last_of(z2, GROUP - 1), edge)
        return links, from_one, from_two

    def backward_flags():
        z1 = jnp.minimum(z + 1, LINES - 1)
        z2 = jnp.minimum(z + 2, LINES - 1)
        edge = first_of(z1, 0)
        links = [None] * GROUP
        links[GROUP - 1] = flag(first_of(z, GROUP - 1), edge)
        for i in range(GROUP - 1):
            links[i] = flag(first_of(z, i), first_of(z, i + 1))
        from_one = jnp.where(z <= LINES - 2, 1.0, 0.0)
        from_two = jnp.where(z <= LINES - 3, 1.0, 0.0) * flag(first_of(z2, 0), edge)
        return links, from_one, from_two

    def line_total(j, landed, mine_r, far, steps, links, stage, slot, direction):
        run = landed[j, steps[0]].astype(F32)
        for i in steps[1:]:
            run = landed[j, i].astype(F32) + links[i] * run
        mine_r[j] = run.astype(BF16)
        for n in (0, 1):
            zt = lax.rem(z + LINES + direction * (n + 1), LINES)
            send(mine_r.at[j], far.at[j, n], stage, slot, ctx_of(zt, g), y)

    def line_carry(j, landed, far, steps, flags, out, back, stage, slot, recv_slot):
        links, from_one, from_two = flags
        took(far.at[j], recv_slot)
        run = from_one * far[j, 0].astype(F32) + from_two * far[j, 1].astype(F32)
        out[j, steps[0]] = run.astype(BF16)
        for n in range(GROUP - 1):
            i = steps[n]
            run = landed[j, i].astype(F32) + links[i] * run
            out[j, steps[n + 1]] = run.astype(BF16)
        for dg in G_ORDER:
            gt = g_peer(dg)
            send(out.at[j, gt], back.at[j, g], stage, slot, ctx_of(z, gt), y)
        back[j, g] = out[j, g]

    up = tuple(range(GROUP))
    down = tuple(reversed(range(GROUP)))

    def f_total(j):
        took(srf.at[j, 0 : GROUP - 1], state_slot + j)
        line_total(j, srf, rf, zrf, up, fwd[0], 4, state_slot + CHUNKS + j, 1)

    def f_carry(j):
        line_carry(j, srf, zrf, up, fwd, csf, crf, 5, state_slot + 2 * CHUNKS + j, state_slot + CHUNKS + j)

    def b_total(j):
        took(srb.at[j, 0 : GROUP - 1], state_slot + 3 * CHUNKS + j)
        line_total(j, srb, rb, zrb, down, bwd[0], 7, state_slot + 4 * CHUNKS + j, -1)

    def b_carry(j):
        line_carry(
            j, srb, zrb, down, bwd, csb, crb, 8, state_slot + 5 * CHUNKS + j, state_slot + 4 * CHUNKS + j
        )

    def carried(ref, j, hh):
        return ref[j, 2 * hh : 2 * hh + 2].reshape(HEAD_DIM, HEAD_DIM)

    def weigh(j):
        for hh in range(CHUNK_HEADS):
            qh, kh = q_of(j, hh), k_of(j, hh)
            weights = (nt(qh, kh) * vis[...]).astype(BF16)
            wt[CHUNK_HEADS * j + hh] = (nt(kh, qh) * vist[...]).astype(BF16)
            kg_part[j, :, lanes_of(hh)] = nn(weights, v_of(j, hh))

    def attend(j):
        took(crf.at[j, 0 : GROUP - 1], state_slot + 2 * CHUNKS + j)
        squares, inner = 0.0, 0.0
        for hh in range(CHUNK_HEADS):
            h = CHUNK_HEADS * j + hh
            cols = slice(HEAD_DIM * h, HEAD_DIM * (h + 1))
            carry = carried(crf, j, hh)
            out = kg_part[j, :, lanes_of(hh)] + resume[...] * nn(q_of(j, hh), carry)
            out = out.astype(BF16)
            att[j, :, lanes_of(hh)] = out
            out = out.astype(F32)
            scaled = ng[:, cols].astype(F32) * gain[:, cols].astype(F32)
            squares = squares + out * out
            inner = inner + scaled * out
        return squares, inner

    first_hop(0)
    took(seg_line.at[0 : LINES - 1], 0)
    seg_all[g] = seg_line[...]
    for dg in G_ORDER:
        send(seg_line, seg_all.at[g], 9, 1, ctx_of(z, g_peer(dg)), y)
    first_hop(1)
    second_hop(0)
    took(seg_all.at[0 : GROUP - 1], 1)
    fwd = forward_flags()
    bwd = backward_flags()
    before = jnp.maximum(me - 1, 0)
    after = jnp.minimum(me + 1, LINES * GROUP - 1)
    seg_rows = jnp.broadcast_to(seg[...].astype(F32), (ROWS, ROWS)).T
    resume[...] = jnp.where(seg_rows == last_of(lax.div(before, GROUP), lax.rem(before, GROUP)), 1.0, 0.0)
    reaches[...] = jnp.where(seg_rows == first_of(lax.div(after, GROUP), lax.rem(after, GROUP)), 1.0, 0.0)
    first_hop(2)
    second_hop(1)
    forward_state(0)
    first_hop(3)
    second_hop(2)
    f_total(0)
    first_hop(4)
    second_hop(3)
    forward_state(1)
    first_hop(5)
    f_carry(0)
    second_hop(4)
    first_hop(6)
    f_total(1)
    second_hop(5)
    forward_state(2)
    first_hop(7)
    f_carry(1)
    second_hop(6)
    weigh(0)
    first_hop(8)
    f_total(2)
    second_hop(7)
    weigh(1)
    ng_copy.wait()
    sums = [attend(0)]
    second_hop(8)
    weigh(2)
    f_carry(2)
    sums.append(attend(1))
    sums.append(attend(2))

    squares = sums[0][0] + sums[1][0] + sums[2][0]
    inner = sums[0][1] + sums[1][1] + sums[2][1]
    sq_send[0:1, :] = jnp.sum(squares.T, axis=0, keepdims=True)
    sq_send[1:2, :] = jnp.sum(inner.T, axis=0, keepdims=True)
    sq_slot = state_slot + 6 * CHUNKS
    for dy in range(1, HEAD_PEERS):
        send(sq_send, sq_recv.at[y], 10, sq_slot, me, lax.rem(y + dy, HEAD_PEERS))
    sq_recv[y] = sq_send[...]
    took(sq_recv.at[0 : HEAD_PEERS - 1], sq_slot)
    total = (sq_recv[0] + sq_recv[1]) + (sq_recv[2] + sq_recv[3])
    width = HEADS * HEAD_DIM
    inverse = lax.rsqrt(total[0:1, :] / width + 1e-05)
    projection = inverse * total[1:2, :] / width
    inverse = jnp.broadcast_to(inverse, (ROWS, ROWS)).T
    projection = jnp.broadcast_to(projection, (ROWS, ROWS)).T

    outs = []

    def put(ref, hbm, j, n):
        copy = pltpu.make_async_copy(ref.at[j], hbm.at[:, WIDE * j : WIDE * (j + 1)], out_sem.at[n, j])
        copy.start()
        outs.append(copy)

    for j in range(CHUNKS):
        for hh in range(CHUNK_HEADS):
            h = CHUNK_HEADS * j + hh
            cols = slice(HEAD_DIM * h, HEAD_DIM * (h + 1))
            gain_f = gain[:, cols].astype(F32)
            scaled = ng[:, cols].astype(F32) * gain_f
            normal = att[j, :, lanes_of(hh)].astype(F32) * inverse
            o_n[j, :, lanes_of(hh)] = (normal * gain_f).astype(BF16)
            gr[j, :, lanes_of(hh)] = (inverse * (scaled - normal * projection)).astype(BF16)
        backward_state(j)
    for j in range(CHUNKS):
        put(o_n, normed_hbm, j, 0)

    def partial(j):
        for hh in range(CHUNK_HEADS):
            h = CHUNK_HEADS * j + hh
            qh, kh, vh = q_of(j, hh), k_of(j, hh), v_of(j, hh)
            gh = gr[j, :, lanes_of(hh)]
            grads = (nt(gh, vh) * vis[...]).astype(BF16)
            grads_t = (nt(vh, gh) * vist[...]).astype(BF16)
            query = nn(grads, kh) + resume[...] * nt(gh, carried(crf, j, hh))
            o_q[j, :, lanes_of(hh)] = query.astype(BF16)
            kg_part[j, :, lanes_of(hh)] = nn(grads_t, qh)
            vg_part[j, :, lanes_of(hh)] = nn(wt[h], gh)
        put(o_q, qg_hbm, j, 1)

    def finish(j):
        took(crb.at[j, 0 : GROUP - 1], state_slot + 5 * CHUNKS + j)
        for hh in range(CHUNK_HEADS):
            back = carried(crb, j, hh)
            key = kg_part[j, :, lanes_of(hh)] + reaches[...] * nt(v_of(j, hh), back)
            o_k[j, :, lanes_of(hh)] = key.astype(BF16)
            value = vg_part[j, :, lanes_of(hh)] + reaches[...] * nn(k_of(j, hh), back)
            o_v[j, :, lanes_of(hh)] = value.astype(BF16)
        put(o_k, kg_hbm, j, 2)
        put(o_v, vg_hbm, j, 3)

    partial(0)
    b_total(0)
    partial(1)
    b_total(1)
    partial(2)
    b_total(2)
    for j in range(CHUNKS):
        b_carry(j)
    for j in range(CHUNKS):
        finish(j)

    def left(ref, stage):
        pltpu.make_async_copy(ref, ref, send_sem.at[stage]).wait()

    left(seg_line.at[0 : LINES - 1], 0)
    left(a.at[:, 0 : ROWS - BAND], 1)
    left(c.at[:, 0 : ROWS - BAND], 2)
    left(sf.at[:, 0 : GROUP - 1], 3)
    left(zrf, 4)
    left(csf.at[:, 0 : GROUP - 1], 5)
    left(sb.at[:, 0 : GROUP - 1], 6)
    left(zrb, 7)
    left(csb.at[:, 0 : GROUP - 1], 8)
    left(seg_all.at[0 : GROUP - 1], 9)
    left(sq_recv.at[0 : HEAD_PEERS - 1], 10)
    for copy in outs:
        copy.wait()


def shards(queries, keys, values, normed_grad, gain, segment, plan):
    vm = pltpu.VMEM
    parcels = vm((PARCELS, ROWS, WIDE), BF16)
    square = vm((ROWS, ROWS), F32)
    square_b = vm((ROWS, ROWS), BF16)
    chunked = vm((CHUNKS, ROWS, WIDE), BF16)
    chunked_f = vm((CHUNKS, ROWS, WIDE), F32)
    states = vm((CHUNKS, GROUP, SLICE, HEAD_DIM), BF16)
    state_set = [
        states, states, vm((CHUNKS, SLICE, HEAD_DIM), BF16), vm((CHUNKS, 2, SLICE, HEAD_DIM), BF16),
        states, states,
    ]
    weights = vm((OWN_HEADS, ROWS, ROWS), BF16)
    sums = vm((8, ROWS), F32)
    out = jax.ShapeDtypeStruct(queries.shape, BF16)
    return tuple(pl.pallas_call(
        kernel,
        out_shape=(out, out, out, out),
        in_specs=[pl.BlockSpec(memory_space=pl.ANY)] * 7,
        out_specs=[pl.BlockSpec(memory_space=pl.ANY)] * 4,
        scratch_shapes=[
            parcels, parcels, parcels, parcels, parcels, parcels,
            vm((ROWS, OWN_HEADS * HEAD_DIM), BF16), vm((1, OWN_HEADS * HEAD_DIM), BF16),
            vm((1, ROWS), jnp.int32), vm((LINES * GROUP, ROWS), jnp.int32),
            vm((LINES, 2, ROWS), F32), vm((GROUP, LINES, 2, ROWS), F32),
            square_b, square_b, square, square, square_b, square_b, square, square,
            *state_set, *state_set,
            chunked, chunked, weights, weights, sums, vm((HEAD_PEERS, 8, ROWS), F32),
            chunked_f, chunked_f, chunked, chunked, chunked, chunked,
            pltpu.SemaphoreType.DMA((PARCELS + 4,)),
            pltpu.SemaphoreType.DMA((4, CHUNKS)),
            pltpu.SemaphoreType.DMA((2,)),
            pltpu.SemaphoreType.DMA((11,)),
            pltpu.SemaphoreType.DMA((2 + 2 * PARCELS + 6 * CHUNKS + 1,)),
        ],
        compiler_params=pltpu.CompilerParams(
            collective_id=0, has_side_effects=True, vmem_limit_bytes=48 << 20
        ),
    )(
        queries, keys, values, normed_grad,
        gain.reshape(1, -1), segment.reshape(1, -1), plan.reshape(LINES * GROUP, ROWS),
    ))


def solution(mesh):
    both = P("ctx", "head")
    return jax.shard_map(
        shards,
        mesh=mesh,
        in_specs=(both, both, both, both, P("head"), P("ctx"), P()),
        out_specs=(both, both, both, both),
        check_vma=False,
    )
```

time: 1160 us -> 82.7 us (0.07); the launches traced: 1140 us -> 82.4 us
  waiting for transfers between devices: 518 us -> 0 us
  loops' own time: 244 us -> 0 us
  blocking collectives: 169 us -> 0 us
  other arithmetic: 111 us -> 0 us
  Pallas kernels: 0 us -> 73.3 us
  local copies, waits for them, and re-layouts: 66.8 us -> 8.42 us
  between operations: 14.3 us -> 0.66 us
    all_gather x2 -> x0, waiting for transfers between devices: 494 us -> none  [entering(): lax.all_gather(a.astype(kind), axis)]
    another operation x2 -> x0, loops' own time: 244 us -> none  [entering(): return lax.fori_loop(0, ahead, one, state)]
    unnamed x1 -> x0, blocking collectives: 126 us -> none
    select_n x69 -> x0, other arithmetic: 105 us -> none  [the longest x63 101 us: pick_joined(): jnp.where(empty_first, second_leaf, jnp.where(empty_second, first_leaf, j...]
    pallas_call x0 -> x1, Pallas kernels: none -> 73.3 us  [shards(): pl.pallas_call(kernel, out_shape=(out, out, out, out), in_specs=[pl.Block...]
    dynamic_slice x63 -> x0, local copies, waits for them, and re-layouts: 38.8 us -> none  [one(): lax.dynamic_index_in_dim(a, source, 0, False).astype(own.dtype)]
    all_to_all x1 -> x0, blocking collectives: 27.9 us -> none  [shards(): lax.all_to_all(outgoing(values), 'ctx', split_axis=0, concat_axis=0, tile...]
    all_to_all x2 -> x0, waiting for transfers between devices: 24 us -> none  [the longest x1 15.1 us: shards(): lax.all_to_all(outgoing(queries), 'ctx', split_axis=0, concat_axis=0, til...]
  transfers between devices with their start and end apart: 4 -> 0, of which waited for: 3 -> 0; matrix products, arithmetic and copies ran while one was open for 2% -> 0% of each run, Pallas kernels for 0% -> 0%
where the time goes in v1:
time: 82.7 us; the launch traced here: 82.4 us
  Pallas kernels  73.3 us (89%)
  local copies, waits for them, and re-layouts  8.42 us (10%)
    pallas_call x1, Pallas kernels, shards(): pl.pallas_call(kernel, out_shape=(out, out, out, out), in_specs=[pl.Block...  73.3 us
    unnamed x16, local copies, waits for them, and re-layouts  7.72 us

profile of v1, /device:TPU:1, one launch (start us, length us, event | category | flops | bytes accessed | tf_op | source)
XLA Modules:
  0.0 82.4 jit_solution(15533299211067767405)
XLA Ops:
  0.6 0.0 copy-start.5
  0.6 0.7 reshape.17.gain_hbm
  1.3 0.0 copy-done.5
  1.3 0.0 copy-start
  1.3 1.0 %copy-done = bf16[128,1536]{1,0:T(8,128)(2,1)S(1)} copy-done((bf16[128,1536]{1,0:T(8,128)(2,1)S(1)}, bf16[128,1536]{1,0:T(8,128)(2,1)}, u32[]{:S(2)}) %copy-start) | copy-done | bytes 393240
  2.3 0.0 copy-start.1
  2.3 1.0 %copy-done.1 = bf16[128,1536]{1,0:T(8,128)(2,1)S(1)} copy-done((bf16[128,1536]{1,0:T(8,128)(2,1)S(1)}, bf16[128,1536]{1,0:T(8,128)(2,1)}, u32[]{:S(2)}) %copy-start.1) | copy-done | bytes 393240
  3.3 0.0 copy-start.2
  3.3 1.0 %copy-done.2 = bf16[128,1536]{1,0:T(8,128)(2,1)S(1)} copy-done((bf16[128,1536]{1,0:T(8,128)(2,1)S(1)}, bf16[128,1536]{1,0:T(8,128)(2,1)}, u32[]{:S(2)}) %copy-start.2) | copy-done | bytes 393240
  4.3 0.0 copy-start.3
  4.3 1.0 %copy-done.3 = bf16[128,1536]{1,0:T(8,128)(2,1)S(1)} copy-done((bf16[128,1536]{1,0:T(8,128)(2,1)S(1)}, bf16[128,1536]{1,0:T(8,128)(2,1)}, u32[]{:S(2)}) %copy-start.3) | copy-done | bytes 393240
  5.3 0.0 copy-start.4
  5.3 0.8 copy-done.4
  6.1 73.3 %shard_map.102 = (bf16[128,1536]{1,0:T(8,128)(2,1)S(1)}, bf16[128,1536]{1,0:T(8,128)(2,1)S(1)}, bf16[128,1536]{1,0:T(8,128)(2,1)S(1)}, bf16[128,1536]{1,0:T(8,128)(2,1)S(1)}) custom-call(bf16[128,1536]{1,0:T(8,128)(2,1)S(1)} %copy-done, bf16[128,1536]{1,0:T(8,128)(2,1)S(1)} %copy-done.1, bf16[128,1536]{1,0:T(8,128)(2,1)S(1)} %copy-done.2, ...), custom_call_target="tpu_custom_call" | custom-call | tf_op jit(solution)/shard_map/pallas_call | solution.py:453
  79.4 0.7 copy.15
  80.1 0.7 copy.16
  80.9 0.7 copy.17
  81.6 0.7 copy.18
Async XLA Ops:
  0.6 0.7 copy-start.5
  1.3 1.0 %copy-start = (bf16[128,1536]{1,0:T(8,128)(2,1)S(1)}, bf16[128,1536]{1,0:T(8,128)(2,1)}, u32[]{:S(2)}) copy-start(bf16[128,1536]{1,0:T(8,128)(2,1)} %q_hbm.1) | copy-start | bytes 1179652
  2.3 1.0 %copy-start.1 = (bf16[128,1536]{1,0:T(8,128)(2,1)S(1)}, bf16[128,1536]{1,0:T(8,128)(2,1)}, u32[]{:S(2)}) copy-start(bf16[128,1536]{1,0:T(8,128)(2,1)} %k_hbm.1) | copy-start | bytes 1179652
  3.3 1.0 %copy-start.2 = (bf16[128,1536]{1,0:T(8,128)(2,1)S(1)}, bf16[128,1536]{1,0:T(8,128)(2,1)}, u32[]{:S(2)}) copy-start(bf16[128,1536]{1,0:T(8,128)(2,1)} %v_hbm.1) | copy-start | bytes 1179652
  4.3 1.0 %copy-start.3 = (bf16[128,1536]{1,0:T(8,128)(2,1)S(1)}, bf16[128,1536]{1,0:T(8,128)(2,1)}, u32[]{:S(2)}) copy-start(bf16[128,1536]{1,0:T(8,128)(2,1)} %ng_hbm.1) | copy-start | bytes 1179652
  5.3 0.8 copy-start.4

commit v2 on v1

--- a/solution.py
+++ b/solution.py
@@ -43,12 +43,12 @@
 
 def kernel(
     q_hbm, k_hbm, v_hbm, ng_hbm, gain_hbm, seg_hbm, plan_hbm,
-    normed_hbm, qg_hbm, kg_hbm, vg_hbm,
+    o_n, o_q, o_k, o_v,
     x, a, b, c, d, seq, ng, gain, seg, plan,
     seg_line, seg_all, mid, settle, vis, vist, tails, heads, resume, reaches,
     sf, srf, rf, zrf, csf, crf, sb, srb, rb, zrb, csb, crb,
-    att, gr, wt, gwt, sq_send, sq_recv, kg_part, vg_part, o_n, o_q, o_k, o_v,
-    load_sem, out_sem, seg_sem, send_sem, recv_sem,
+    att, gr, wt, sq_send, sq_recv, kg_part, vg_part,
+    load_sem, send_sem, recv_sem,
 ):
     me = lax.axis_index("ctx")
     y = lax.axis_index("head")
@@ -75,27 +75,6 @@
 
     def took(ref, slot):
         pltpu.make_async_copy(ref, ref, recv_sem.at[slot]).wait()
-
-    order = []
-    for j in range(CHUNKS):
-        order.append((k_hbm, j))
-        order.append((v_hbm, j))
-    for j in range(CHUNKS):
-        order.append((q_hbm, j))
-    small = [
-        pltpu.make_async_copy(plan_hbm, plan, load_sem.at[PARCELS]),
-        pltpu.make_async_copy(seg_hbm, seg, load_sem.at[PARCELS + 1]),
-        pltpu.make_async_copy(gain_hbm, gain, load_sem.at[PARCELS + 2]),
-    ]
-    for copy in small:
-        copy.start()
-    loads = []
-    for p, (ref, j) in enumerate(order):
-        copy = pltpu.make_async_copy(ref.at[:, WIDE * j : WIDE * (j + 1)], x.at[p], load_sem.at[p])
-        copy.start()
-        loads.append(copy)
-    ng_copy = pltpu.make_async_copy(ng_hbm, ng, load_sem.at[PARCELS + 3])
-    ng_copy.start()
 
     barrier = pltpu.get_barrier_semaphore()
     for dz in Z_ORDER:
@@ -107,40 +86,69 @@
             barrier, inc=1, device_id=(me, lax.rem(y + dy, HEAD_PEERS)), device_id_type=MESH
         )
 
-    for copy in small:
-        copy.wait()
+    order = []
+    for j in range(CHUNKS):
+        order.append((k_hbm, j))
+        order.append((v_hbm, j))
+    for j in range(CHUNKS):
+        order.append((q_hbm, j))
+    plan_copy = pltpu.make_async_copy(plan_hbm, plan, load_sem.at[PARCELS])
+    plan_copy.start()
+    seg_copy = pltpu.make_async_copy(seg_hbm, seg, load_sem.at[PARCELS + 1])
+    seg_copy.start()
+    loads = []
+    for p, (ref, j) in enumerate(order):
+        copy = pltpu.make_async_copy(ref.at[:, WIDE * j : WIDE * (j + 1)], x.at[p], load_sem.at[p])
+        copy.start()
+        loads.append(copy)
+    gain_copy = pltpu.make_async_copy(gain_hbm, gain, load_sem.at[PARCELS + 2])
+    gain_copy.start()
+    ng_copy = pltpu.make_async_copy(ng_hbm, ng, load_sem.at[PARCELS + 3])
+    ng_copy.start()
+
+    plan_copy.wait()
     rows_i = iota(0)
     cols_i = iota(1)
     own_plan = plan[pl.ds(me, 1), :]
     slot_of = 2 * lax.shift_right_logical(own_plan, 7) + (cols_i[0:1, :] & 1)
     leave = (rows_i == slot_of).astype(F32).astype(BF16)
-    for p in range(PARCELS):
+
+    def sort(p):
         loads[p].wait()
         a[p] = nn(leave, x[p]).astype(BF16)
 
-    seg_row = seg[...]
-    seg_f = seg_row.astype(F32)
+    def depart(p):
+        for dz in Z_ORDER:
+            zt = z_peer(dz)
+            send(a.at[p, band(zt)], b.at[p, band(z)], 1, 2 + p, ctx_of(zt, g), y)
+        b[p, band(z), :] = a[p, band(z), :]
+
+    seg_copy.wait()
+    seg_f = seg[...].astype(F32)
+    last_here = jnp.broadcast_to(seg_f[:, ROWS - 1 : ROWS], (1, ROWS))
+    first_here = jnp.broadcast_to(seg_f[:, 0:1], (1, ROWS))
+    seg_line[z, 0:1, :] = last_here
+    seg_line[z, 1:2, :] = first_here
+    sort(0)
+
+    pl.semaphore_wait(barrier, LINES - 1 + GROUP - 1 + HEAD_PEERS - 1)
+
+    depart(0)
+    for dz in Z_ORDER:
+        send(seg_line.at[z], seg_line.at[z], 0, 0, ctx_of(z_peer(dz), g), y)
+    for p in range(1, 2 * CHUNKS + 1):
+        sort(p)
+        depart(p)
+    for p in range(2 * CHUNKS + 1, PARCELS):
+        sort(p)
+
     seg_lanes = jnp.broadcast_to(seg_f, (ROWS, ROWS))
     seg_rows = seg_lanes.T
-    last_here = jnp.broadcast_to(seg_f[:, ROWS - 1 : ROWS], (1, ROWS))
-    first_here = jnp.broadcast_to(seg_f[:, 0:1], (1, ROWS))
     same = seg_lanes == seg_rows
     vis[...] = jnp.where(same & (rows_i >= cols_i), 1.0, 0.0)
     vist[...] = jnp.where(same & (cols_i >= rows_i), 1.0, 0.0)
     tails[...] = jnp.where(seg_rows == last_here, 1.0, 0.0).astype(BF16)
     heads[...] = jnp.where(seg_rows == first_here, 1.0, 0.0).astype(BF16)
-    seg_line[z, 0:1, :] = last_here
-    seg_line[z, 1:2, :] = first_here
-
-    pl.semaphore_wait(barrier, LINES - 1 + GROUP - 1 + HEAD_PEERS - 1)
-
-    for dz in Z_ORDER:
-        send(seg_line.at[z], seg_line.at[z], 0, 0, ctx_of(z_peer(dz), g), y)
-    for p in range(PARCELS):
-        for dz in Z_ORDER:
-            zt = z_peer(dz)
-            send(a.at[p, band(zt)], b.at[p, band(z)], 1, 2 + p, ctx_of(zt, g), y)
-        b[p, band(z), :] = a[p, band(z), :]
 
     source = ((rows_i & 15) >> 1) * BAND + (rows_i >> 4) * 2 + (rows_i & 1)
     mid[...] = (cols_i == source).astype(F32).astype(BF16)
@@ -319,31 +327,34 @@
     forward_state(0)
     first_hop(3)
     second_hop(2)
+    first_hop(4)
     f_total(0)
-    first_hop(4)
+    depart(7)
     second_hop(3)
     forward_state(1)
     first_hop(5)
+    second_hop(4)
+    f_total(1)
+    depart(8)
     f_carry(0)
-    second_hop(4)
     first_hop(6)
-    f_total(1)
     second_hop(5)
     forward_state(2)
-    first_hop(7)
     f_carry(1)
     second_hop(6)
     weigh(0)
-    first_hop(8)
+    first_hop(7)
     f_total(2)
+    gain_copy.wait()
+    ng_copy.wait()
+    sums = [attend(0)]
     second_hop(7)
     weigh(1)
-    ng_copy.wait()
-    sums = [attend(0)]
+    first_hop(8)
+    f_carry(2)
+    sums.append(attend(1))
     second_hop(8)
     weigh(2)
-    f_carry(2)
-    sums.append(attend(1))
     sums.append(attend(2))
 
     squares = sums[0][0] + sums[1][0] + sums[2][0]
@@ -362,25 +373,21 @@
     inverse = jnp.broadcast_to(inverse, (ROWS, ROWS)).T
     projection = jnp.broadcast_to(projection, (ROWS, ROWS)).T
 
-    outs = []
-
-    def put(ref, hbm, j, n):
-        copy = pltpu.make_async_copy(ref.at[j], hbm.at[:, WIDE * j : WIDE * (j + 1)], out_sem.at[n, j])
-        copy.start()
-        outs.append(copy)
-
     for j in range(CHUNKS):
         for hh in range(CHUNK_HEADS):
             h = CHUNK_HEADS * j + hh
             cols = slice(HEAD_DIM * h, HEAD_DIM * (h + 1))
-            gain_f = gain[:, cols].astype(F32)
-            scaled = ng[:, cols].astype(F32) * gain_f
+            scaled = ng[:, cols].astype(F32) * gain[:, cols].astype(F32)
             normal = att[j, :, lanes_of(hh)].astype(F32) * inverse
-            o_n[j, :, lanes_of(hh)] = (normal * gain_f).astype(BF16)
             gr[j, :, lanes_of(hh)] = (inverse * (scaled - normal * projection)).astype(BF16)
         backward_state(j)
-    for j in range(CHUNKS):
-        put(o_n, normed_hbm, j, 0)
+
+    def norm(j):
+        for hh in range(CHUNK_HEADS):
+            h = CHUNK_HEADS * j + hh
+            normal = att[j, :, lanes_of(hh)].astype(F32) * inverse
+            gain_f = gain[:, HEAD_DIM * h : HEAD_DIM * (h + 1)].astype(F32)
+            o_n[j, :, lanes_of(hh)] = (normal * gain_f).astype(BF16)
 
     def partial(j):
         for hh in range(CHUNK_HEADS):
@@ -393,7 +400,6 @@
             o_q[j, :, lanes_of(hh)] = query.astype(BF16)
             kg_part[j, :, lanes_of(hh)] = nn(grads_t, qh)
             vg_part[j, :, lanes_of(hh)] = nn(wt[h], gh)
-        put(o_q, qg_hbm, j, 1)
 
     def finish(j):
         took(crb.at[j, 0 : GROUP - 1], state_slot + 5 * CHUNKS + j)
@@ -403,15 +409,16 @@
             o_k[j, :, lanes_of(hh)] = key.astype(BF16)
             value = vg_part[j, :, lanes_of(hh)] + reaches[...] * nn(k_of(j, hh), back)
             o_v[j, :, lanes_of(hh)] = value.astype(BF16)
-        put(o_k, kg_hbm, j, 2)
-        put(o_v, vg_hbm, j, 3)
-
+
+    norm(0)
+    norm(1)
+    norm(2)
     partial(0)
+    partial(1)
     b_total(0)
-    partial(1)
     b_total(1)
+    b_total(2)
     partial(2)
-    b_total(2)
     for j in range(CHUNKS):
         b_carry(j)
     for j in range(CHUNKS):
@@ -431,7 +438,16 @@
     left(csb.at[:, 0 : GROUP - 1], 8)
     left(seg_all.at[0 : GROUP - 1], 9)
     left(sq_recv.at[0 : HEAD_PEERS - 1], 10)
-    for copy in outs:
+
+
+def deliver(n_in, q_in, k_in, v_in, n_out, q_out, k_out, v_out, sem):
+    copies = []
+    for i, (src, dst) in enumerate(((n_in, n_out), (q_in, q_out), (k_in, k_out), (v_in, v_out))):
+        for j in range(CHUNKS):
+            copy = pltpu.make_async_copy(src.at[j], dst.at[:, WIDE * j : WIDE * (j + 1)], sem.at[i, j])
+            copy.start()
+            copies.append(copy)
+    for copy in copies:
         copy.wait()
 
 
@@ -449,12 +465,16 @@
     ]
     weights = vm((OWN_HEADS, ROWS, ROWS), BF16)
     sums = vm((8, ROWS), F32)
-    out = jax.ShapeDtypeStruct(queries.shape, BF16)
-    return tuple(pl.pallas_call(
+    out = vm((CHUNKS, ROWS, WIDE), BF16)
+    inputs = (
+        queries, keys, values, normed_grad,
+        gain.reshape(1, -1), segment.reshape(1, -1), plan.reshape(LINES * GROUP, ROWS),
+    )
+    results = pl.pallas_call(
         kernel,
         out_shape=(out, out, out, out),
-        in_specs=[pl.BlockSpec(memory_space=pl.ANY)] * 7,
-        out_specs=[pl.BlockSpec(memory_space=pl.ANY)] * 4,
+        in_specs=[pl.BlockSpec(memory_space=pltpu.HBM)] * 7,
+        out_specs=[pl.BlockSpec(memory_space=pltpu.VMEM)] * 4,
         scratch_shapes=[
             parcels, parcels, parcels, parcels, parcels, parcels,
             vm((ROWS, OWN_HEADS * HEAD_DIM), BF16), vm((1, OWN_HEADS * HEAD_DIM), BF16),
@@ -462,21 +482,24 @@
             vm((LINES, 2, ROWS), F32), vm((GROUP, LINES, 2, ROWS), F32),
             square_b, square_b, square, square, square_b, square_b, square, square,
             *state_set, *state_set,
-            chunked, chunked, weights, weights, sums, vm((HEAD_PEERS, 8, ROWS), F32),
-            chunked_f, chunked_f, chunked, chunked, chunked, chunked,
+            chunked, chunked, weights, sums, vm((HEAD_PEERS, 8, ROWS), F32),
+            chunked_f, chunked_f,
             pltpu.SemaphoreType.DMA((PARCELS + 4,)),
-            pltpu.SemaphoreType.DMA((4, CHUNKS)),
-            pltpu.SemaphoreType.DMA((2,)),
             pltpu.SemaphoreType.DMA((11,)),
             pltpu.SemaphoreType.DMA((2 + 2 * PARCELS + 6 * CHUNKS + 1,)),
         ],
         compiler_params=pltpu.CompilerParams(
-            collective_id=0, has_side_effects=True, vmem_limit_bytes=48 << 20
+            collective_id=0, has_side_effects=True, vmem_limit_bytes=40 << 20
         ),
-    )(
-        queries, keys, values, normed_grad,
-        gain.reshape(1, -1), segment.reshape(1, -1), plan.reshape(LINES * GROUP, ROWS),
-    ))
+    )(*(pltpu.with_memory_space_constraint(t, pltpu.HBM) for t in inputs))
+    final = jax.ShapeDtypeStruct(queries.shape, BF16)
+    return tuple(pl.pallas_call(
+        deliver,
+        out_shape=(final, final, final, final),
+        in_specs=[pl.BlockSpec(memory_space=pltpu.VMEM)] * 4,
+        out_specs=[pl.BlockSpec(memory_space=pltpu.HBM)] * 4,
+        scratch_shapes=[pltpu.SemaphoreType.DMA((4, CHUNKS))],
+    )(*(pltpu.with_memory_space_constraint(t, pltpu.VMEM) for t in results)))
 
 
 def solution(mesh):

time: 82.7 us -> 72.5 us (0.88)
  local copies, waits for them, and re-layouts: 8.42 us -> 1.28 us
  Pallas kernels: 73.3 us -> 70.4 us
    unnamed x16 -> x0, local copies, waits for them, and re-layouts: 7.72 us -> none
    pallas_call x1, Pallas kernels: 73.3 us -> 69.2 us  [shards(): pl.pallas_call(kernel, out_shape=(out, out, out, out), in_specs=[pl.Block...]
    pallas_call x0 -> x1, Pallas kernels: none -> 1.24 us  [shards(): pl.pallas_call(deliver, out_shape=(final, final, final, final), in_specs=...]
where the time goes in v2:
time: 72.5 us; the launch traced here: 72.3 us
  Pallas kernels  70.4 us (97%)
  local copies, waits for them, and re-layouts  1.28 us (2%)
    pallas_call x1, Pallas kernels, shards(): pl.pallas_call(kernel, out_shape=(out, out, out, out), in_specs=[pl.Block...  69.2 us

profile of v2, /device:TPU:1, one launch (start us, length us, event | category | flops | bytes accessed | tf_op | source)
XLA Modules:
  0.0 72.3 jit_solution(17030611775717713614)
XLA Ops:
  0.6 1.3 %reshape.17.gain_hbm = bf16[1,1536]{1,0:T(2,128)(2,1)} reshape(bf16[1536]{0:T(1024)(128)(2,1)} %param.11) | data formatting | bytes 6144 | tf_op jit(solution)/shard_map/reshape | solution.py:471
  1.9 69.2 %shard_map.102 = (bf16[3,128,512]{2,1,0:T(8,128)(2,1)S(1)}, bf16[3,128,512]{2,1,0:T(8,128)(2,1)S(1)}, bf16[3,128,512]{2,1,0:T(8,128)(2,1)S(1)}, bf16[3,128,512]{2,1,0:T(8,128)(2,1)S(1)}) custom-call(bf16[128,1536]{1,0:T(8,128)(2,1)} %q_hbm.1, bf16[128,1536]{1,0:T(8,128)(2,1)} %k_hbm.1, bf16[128,1536]{1,0:T(8,128)(2,1)} %v_hbm.1, bf16[128,1536]{1,0:T(8,128)(2,1)} %ng_hbm.1, ...), custom_call_target="tpu_custom_call" | custom-call | tf_op jit(solution)/shard_map/pallas_call | solution.py:473
  71.1 1.2 %shard_map.103 = (bf16[128,1536]{1,0:T(8,128)(2,1)}, bf16[128,1536]{1,0:T(8,128)(2,1)}, bf16[128,1536]{1,0:T(8,128)(2,1)}, bf16[128,1536]{1,0:T(8,128)(2,1)}) custom-call(bf16[3,128,512]{2,1,0:T(8,128)(2,1)S(1)} %get-tuple-element.8.n_in, bf16[3,128,512]{2,1,0:T(8,128)(2,1)S(1)} %get-tuple-element.9.q_in, bf16[3,128,512]{2,1,0:T(8,128)(2,1)S(1)} %get-tuple-element.10.k_in, ...), custom_call_target="tpu_custom_call" | custom-call | tf_op jit(solution)/shard_map/pallas_call | solution.py:496

commit v3 on v2

v3 whole, which is shorter than its diff:
```python
import jax
import jax.numpy as jnp
from jax import lax
from jax.experimental import pallas as pl
from jax.experimental.pallas import tpu as pltpu
from jax.sharding import PartitionSpec as P

HEADS = 48
HEAD_DIM = 128
ROWS = 128
LINES = 8
GROUP = 8
OWN_HEADS = 12
AHEAD = (4, 4, 3, 1)
BACK = (2, 4, 4, 2)
BAND = ROWS // LINES
PIECE = HEAD_DIM // GROUP
HEAD_PEERS = 4
MESH = pl.DeviceIdType.MESH
F32 = jnp.float32
BF16 = jnp.bfloat16
Z_ORDER = (4, 3, 5, 2, 6, 1, 7)
G_ORDER = (4, 3, 5, 2, 6, 1, 7)

KEY, VALUE, QUERY = 0, 1, 2
PARCELS = [(t, j) for j in range(len(AHEAD)) for t in (KEY, VALUE)]
PARCELS += [(QUERY, j) for j in range(len(AHEAD))]


def spans(chunks):
    firsts = [sum(chunks[:j]) for j in range(len(chunks))]
    return [range(f, f + n) for f, n in zip(firsts, chunks)]


AHEAD_SPANS = spans(AHEAD)
BACK_SPANS = spans(BACK)
PLACE = {h: (j, h - span[0]) for j, span in enumerate(AHEAD_SPANS) for h in span}


def timeline():
    wire_z, late_z, wire_x, late_x, wire_line, late_line = 0.7, 4.0, 0.36, 3.5, 0.2, 3.3
    events, second, clock = [], {}, 0.0
    for p, (t, j) in enumerate(PARCELS):
        clock += wire_z * AHEAD[j]
        first = clock + late_z
        events.append((first, "first_hop", p))
        second[t, j] = first + late_x + wire_x * AHEAD[j]
        events.append((second[t, j], "second_hop", p))
    for j, heads in enumerate(AHEAD):
        ready = second[VALUE, j] + 0.01
        events.append((ready, "forward_state", j))
        ready += late_x + (wire_x + 0.1) * heads
        events.append((ready, "f_total", j))
        clock = max(clock, ready) + wire_line * heads
        ready = clock + late_line
        events.append((ready, "f_carry", j))
        ready = max(ready + late_x + wire_x * heads, second[QUERY, j] + 0.02)
        events.append((second[QUERY, j] + 0.01, "weigh", j))
        events.append((ready, "attend", j))
    return [event[1:] for event in sorted(events)]


def nn(a, b):
    return lax.dot_general(a, b, (((1,), (0,)), ((), ())), preferred_element_type=F32)


def nt(a, b):
    return lax.dot_general(a, b, (((1,), (1,)), ((), ())), preferred_element_type=F32)


def tn(a, b):
    return lax.dot_general(a, b, (((0,), (0,)), ((), ())), preferred_element_type=F32)


def iota(dim):
    return lax.broadcasted_iota(jnp.int32, (ROWS, ROWS), dim)


def kernel(
    q_hbm, k_hbm, v_hbm, ng_hbm, gain_hbm, seg_hbm, plan_hbm,
    o_n, o_q, o_k, o_v,
    x, a, b, c, d, seq, ng, gain, gain_rows, seg, plan,
    seg_line, seg_all, mid, settle, vis, vist, tails, heads, resume, reaches,
    sf, srf, rf, zrf, csf, crf, sb, srb, rb, zrb, csb, crb,
    att, gr, wt, sq_send, sq_recv, kg_part, vg_part,
    load_sem, send_sem, hop_sem, state_sem, small_sem,
):
    me = lax.axis_index("ctx")
    y = lax.axis_index("head")
    z = lax.div(me, GROUP)
    g = lax.rem(me, GROUP)

    def z_peer(dz):
        return lax.rem(z + dz, LINES)

    def g_peer(dg):
        return lax.rem(g + dg, GROUP)

    def ctx_of(zz, gg):
        return zz * GROUP + gg

    def band(i):
        return pl.ds(pl.multiple_of(i * BAND, BAND), BAND)

    def send(src, dst, stage, sem, ctx_to, head_to):
        pltpu.make_async_remote_copy(
            src_ref=src, dst_ref=dst, send_sem=send_sem.at[stage], recv_sem=sem,
            device_id=(ctx_to, head_to), device_id_type=MESH,
        ).start()

    def took(ref, sem):
        pltpu.make_async_copy(ref, ref, sem).wait()

    barrier = pltpu.get_barrier_semaphore()
    for dz in Z_ORDER:
        pl.semaphore_signal(barrier, inc=1, device_id=(ctx_of(z_peer(dz), g), y), device_id_type=MESH)
    for dg in G_ORDER:
        pl.semaphore_signal(barrier, inc=1, device_id=(ctx_of(z, g_peer(dg)), y), device_id_type=MESH)
    for dy in range(1, HEAD_PEERS):
        pl.semaphore_signal(
            barrier, inc=1, device_id=(me, lax.rem(y + dy, HEAD_PEERS)), device_id_type=MESH
        )

    plan_copy = pltpu.make_async_copy(plan_hbm, plan, load_sem.at[len(PARCELS)])
    plan_copy.start()
    seg_copy = pltpu.make_async_copy(seg_hbm, seg, load_sem.at[len(PARCELS) + 1])
    seg_copy.start()
    loads = []
    for p, (t, j) in enumerate(PARCELS):
        span = AHEAD_SPANS[j]
        cols = slice(span.start * HEAD_DIM, span.stop * HEAD_DIM)
        copy = pltpu.make_async_copy((k_hbm, v_hbm, q_hbm)[t].at[:, cols], x[j].at[t], load_sem.at[p])
        copy.start()
        loads.append(copy)
    gain_copy = pltpu.make_async_copy(gain_hbm, gain, load_sem.at[len(PARCELS) + 2])
    gain_copy.start()
    ng_copy = pltpu.make_async_copy(ng_hbm, ng, load_sem.at[len(PARCELS) + 3])
    ng_copy.start()

    plan_copy.wait()
    rows_i = iota(0)
    cols_i = iota(1)
    own_plan = plan[pl.ds(me, 1), :]
    slot_of = 2 * lax.shift_right_logical(own_plan, 7) + (cols_i[0:1, :] & 1)
    leave = (rows_i == slot_of).astype(F32).astype(BF16)

    def sort(p):
        t, j = PARCELS[p]
        loads[p].wait()
        a[j][t] = nn(leave, x[j][t]).astype(BF16)

    def depart(p):
        t, j = PARCELS[p]
        for dz in Z_ORDER:
            zt = z_peer(dz)
            send(a[j].at[t, band(zt)], b[j].at[t, band(z)], 0, hop_sem.at[0, p], ctx_of(zt, g), y)
        b[j][t, band(z), :] = a[j][t, band(z), :]

    seg_copy.wait()
    seg_f = seg[...].astype(F32)
    last_here = jnp.broadcast_to(seg_f[:, ROWS - 1 : ROWS], (1, ROWS))
    first_here = jnp.broadcast_to(seg_f[:, 0:1], (1, ROWS))
    seg_line[z, 0:1, :] = last_here
    seg_line[z, 1:2, :] = first_here
    sort(0)

    pl.semaphore_wait(barrier, LINES - 1 + GROUP - 1 + HEAD_PEERS - 1)

    for dz in Z_ORDER:
        send(seg_line.at[z], seg_line.at[z], 1, small_sem.at[0], ctx_of(z_peer(dz), g), y)
    depart(0)
    for p, (t, j) in enumerate(PARCELS):
        if p > 0:
            sort(p)
            depart(p)

    seg_lanes = jnp.broadcast_to(seg_f, (ROWS, ROWS))
    seg_rows = seg_lanes.T
    same = seg_lanes == seg_rows
    vis[...] = jnp.where(same & (rows_i >= cols_i), 1.0, 0.0)
    vist[...] = jnp.where(same & (cols_i >= rows_i), 1.0, 0.0)
    tails[...] = jnp.where(seg_rows == last_here, 1.0, 0.0).astype(BF16)
    heads[...] = jnp.where(seg_rows == first_here, 1.0, 0.0).astype(BF16)

    source = ((rows_i & 15) >> 1) * BAND + (rows_i >> 4) * 2 + (rows_i & 1)
    mid[...] = (cols_i == source).astype(F32).astype(BF16)
    plan_all = plan[...]
    lanes = lax.broadcasted_iota(jnp.int32, (LINES * GROUP, ROWS), 1)
    mine = (lax.shift_right_logical(plan_all, 7) == me) & ((lanes & 1) == 0)
    start = jnp.sum(jnp.where(mine, (plan_all & 127).astype(F32), 0.0), axis=1, keepdims=True)
    start = jnp.broadcast_to(start, (LINES * GROUP, ROWS)).astype(BF16)
    pick_rows = lax.broadcasted_iota(jnp.int32, (ROWS, LINES * GROUP), 0)
    pick_cols = lax.broadcasted_iota(jnp.int32, (ROWS, LINES * GROUP), 1)
    pick = (pick_cols == ((pick_rows & 15) >> 1) * GROUP + (pick_rows >> 4)).astype(F32).astype(BF16)
    place = nn(pick, start) + (rows_i & 1).astype(F32)
    settle[...] = jnp.where(cols_i.astype(F32) == place, 1.0, 0.0).T.astype(BF16)

    def first_hop(p):
        t, j = PARCELS[p]
        took(b[j].at[t, 0 : ROWS - BAND], hop_sem.at[0, p])
        c[j][t] = nn(mid[...], b[j][t]).astype(BF16)
        for dg in G_ORDER:
            gt = g_peer(dg)
            send(c[j].at[t, band(gt)], d[j].at[t, band(g)], 2, hop_sem.at[1, p], ctx_of(z, gt), y)
        d[j][t, band(g), :] = c[j][t, band(g), :]
        if p == 0:
            took(seg_line.at[0 : LINES - 1], small_sem.at[0])
            seg_all[g] = seg_line[...]
            for dg in G_ORDER:
                send(seg_line, seg_all.at[g], 3, small_sem.at[1], ctx_of(z, g_peer(dg)), y)

    def second_hop(p):
        t, j = PARCELS[p]
        took(d[j].at[t, 0 : ROWS - BAND], hop_sem.at[1, p])
        seq[j][t] = nn(settle[...], d[j][t]).astype(BF16)

    def rows_of(t, h):
        j, hh = PLACE[h]
        return seq[j][t, :, HEAD_DIM * hh : HEAD_DIM * (hh + 1)]

    def columns(h):
        return slice(HEAD_DIM * h, HEAD_DIM * (h + 1))

    def spread(local, landed, stage, sem):
        for dg in G_ORDER:
            gt = g_peer(dg)
            send(local.at[gt], landed.at[g], stage, sem, ctx_of(z, gt), y)
        landed[g] = local[g]

    def forward_state(j):
        for hh, h in enumerate(AHEAD_SPANS[j]):
            state = tn(rows_of(KEY, h) * tails[...], rows_of(VALUE, h)).astype(BF16)
            sf[j][:, hh] = state.reshape(GROUP, PIECE, HEAD_DIM)
        spread(sf[j], srf[j], 4, state_sem.at[0, j])

    def backward_state(j):
        for hh, h in enumerate(BACK_SPANS[j]):
            state = tn(rows_of(QUERY, h) * heads[...], gr[h]).astype(BF16)
            sb[j][:, hh] = state.reshape(GROUP, PIECE, HEAD_DIM)
        spread(sb[j], srb[j], 7, state_sem.at[3, j])

    def last_of(zz, gg):
        return seg_all[gg, zz, 0:1, :]

    def first_of(zz, gg):
        return seg_all[gg, zz, 1:2, :]

    def flag(one, two):
        return jnp.where(one == two, 1.0, 0.0)

    def forward_flags():
        z1 = jnp.maximum(z - 1, 0)
        z2 = jnp.maximum(z - 2, 0)
        edge = last_of(z1, GROUP - 1)
        links = [flag(last_of(z, 0), edge)]
        for i in range(1, GROUP):
            links.append(flag(last_of(z, i), last_of(z, i - 1)))
        from_one = jnp.where(z >= 1, 1.0, 0.0)
        from_two = jnp.where(z >= 2, 1.0, 0.0) * flag(last_of(z2, GROUP - 1), edge)
        return links, from_one, from_two

    def backward_flags():
        z1 = jnp.minimum(z + 1, LINES - 1)
        z2 = jnp.minimum(z + 2, LINES - 1)
        edge = first_of(z1, 0)
        links = [flag(first_of(z, i), first_of(z, i + 1)) for i in range(GROUP - 1)]
        links.append(flag(first_of(z, GROUP - 1), edge))
        from_one = jnp.where(z <= LINES - 2, 1.0, 0.0)
        from_two = jnp.where(z <= LINES - 3, 1.0, 0.0) * flag(first_of(z2, 0), edge)
        return links, from_one, from_two

    def line_total(landed, mine_r, far, steps, links, stage, sem, direction):
        run = landed[steps[0]].astype(F32)
        for i in steps[1:]:
            run = landed[i].astype(F32) + links[i] * run
        mine_r[...] = run.astype(BF16)
        for n in (1, 0):
            zt = lax.rem(z + LINES + direction * (n + 1), LINES)
            send(mine_r, far.at[n], stage, sem, ctx_of(zt, g), y)

    def line_carry(landed, far, steps, flags, out, back, stage, far_sem, back_sem):
        links, from_one, from_two = flags
        took(far, far_sem)
        run = from_one * far[0].astype(F32) + from_two * far[1].astype(F32)
        out[steps[0]] = run.astype(BF16)
        for n in range(GROUP - 1):
            i = steps[n]
            run = landed[i].astype(F32) + links[i] * run
            out[steps[n + 1]] = run.astype(BF16)
        spread(out, back, stage, back_sem)

    up = tuple(range(GROUP))
    down = tuple(reversed(range(GROUP)))
    flags = {}

    def meet():
        gain_copy.wait()
        for h in range(OWN_HEADS):
            gain_rows[h] = gain[columns(h)].astype(F32).reshape(1, HEAD_DIM)
        took(seg_all.at[0 : GROUP - 1], small_sem.at[1])
        flags["ahead"] = forward_flags()
        flags["back"] = backward_flags()
        before = jnp.maximum(me - 1, 0)
        after = jnp.minimum(me + 1, LINES * GROUP - 1)
        here = jnp.broadcast_to(seg[...].astype(F32), (ROWS, ROWS)).T
        resume[...] = jnp.where(here == last_of(lax.div(before, GROUP), lax.rem(before, GROUP)), 1.0, 0.0)
        reaches[...] = jnp.where(here == first_of(lax.div(after, GROUP), lax.rem(after, GROUP)), 1.0, 0.0)

    def f_total(j):
        if not flags:
            meet()
        took(srf[j].at[0 : GROUP - 1], state_sem.at[0, j])
        line_total(srf[j], rf[j], zrf[j], up, flags["ahead"][0], 5, state_sem.at[1, j], 1)

    def f_carry(j):
        line_carry(
            srf[j], zrf[j], up, flags["ahead"], csf[j], crf[j], 6, state_sem.at[1, j], state_sem.at[2, j]
        )

    def b_total(j):
        took(srb[j].at[0 : GROUP - 1], state_sem.at[3, j])
        line_total(srb[j], rb[j], zrb[j], down, flags["back"][0], 8, state_sem.at[4, j], -1)

    def b_carry(j):
        line_carry(
            srb[j], zrb[j], down, flags["back"], csb[j], crb[j], 9, state_sem.at[4, j], state_sem.at[5, j]
        )

    def carried(ref, hh):
        return ref[:, hh].reshape(HEAD_DIM, HEAD_DIM)

    def weigh(j):
        for h in AHEAD_SPANS[j]:
            qh, kh = rows_of(QUERY, h), rows_of(KEY, h)
            weights = (nt(qh, kh) * vis[...]).astype(BF16)
            wt[h] = (nt(kh, qh) * vist[...]).astype(BF16)
            kg_part[h] = nn(weights, rows_of(VALUE, h))

    sums = []

    def attend(j):
        if not sums:
            ng_copy.wait()
        took(crf[j].at[0 : GROUP - 1], state_sem.at[2, j])
        squares, inner = 0.0, 0.0
        for hh, h in enumerate(AHEAD_SPANS[j]):
            out = kg_part[h] + resume[...] * nn(rows_of(QUERY, h), carried(crf[j], hh))
            out = out.astype(BF16)
            att[h] = out
            out = out.astype(F32)
            scaled = ng[:, columns(h)].astype(F32) * gain_rows[h]
            squares = squares + out * out
            inner = inner + scaled * out
        sums.append((squares, inner))

    work = dict(
        first_hop=first_hop, second_hop=second_hop, forward_state=forward_state,
        f_total=f_total, f_carry=f_carry, weigh=weigh, attend=attend,
    )
    for name, n in timeline():
        work[name](n)

    squares = sum(one for one, _ in sums)
    inner = sum(two for _, two in sums)
    sq_send[0:1, :] = jnp.sum(squares.T, axis=0, keepdims=True)
    sq_send[1:2, :] = jnp.sum(inner.T, axis=0, keepdims=True)
    for dy in (2, 1, 3):
        send(sq_send, sq_recv.at[y], 10, small_sem.at[2], me, lax.rem(y + dy, HEAD_PEERS))
    sq_recv[y] = sq_send[...]
    took(sq_recv.at[0 : HEAD_PEERS - 1], small_sem.at[2])
    total = (sq_recv[0] + sq_recv[1]) + (sq_recv[2] + sq_recv[3])
    width = HEADS * HEAD_DIM
    inverse = lax.rsqrt(total[0:1, :] / width + 1e-05)
    projection = inverse * total[1:2, :] / width
    inverse = jnp.broadcast_to(inverse, (ROWS, ROWS)).T
    projection = jnp.broadcast_to(projection, (ROWS, ROWS)).T

    for j, span in enumerate(BACK_SPANS):
        for h in span:
            scaled = ng[:, columns(h)].astype(F32) * gain_rows[h]
            normal = att[h].astype(F32) * inverse
            gr[h] = (inverse * (scaled - normal * projection)).astype(BF16)
        backward_state(j)

    def norm(h):
        normal = att[h].astype(F32) * inverse
        o_n[:, columns(h)] = (normal * gain_rows[h]).astype(BF16)

    def partial(h):
        j, hh = PLACE[h]
        qh, kh, vh, gh = rows_of(QUERY, h), rows_of(KEY, h), rows_of(VALUE, h), gr[h]
        grads = (nt(gh, vh) * vis[...]).astype(BF16)
        grads_t = (nt(vh, gh) * vist[...]).astype(BF16)
        query = nn(grads, kh) + resume[...] * nt(gh, carried(crf[j], hh))
        o_q[:, columns(h)] = query.astype(BF16)
        kg_part[h] = nn(grads_t, qh)
        vg_part[h] = nn(wt[h], gh)

    def finish(j):
        took(crb[j].at[0 : GROUP - 1], state_sem.at[5, j])
        for hh, h in enumerate(BACK_SPANS[j]):
            back = carried(crb[j], hh)
            key = kg_part[h] + reaches[...] * nt(rows_of(VALUE, h), back)
            o_k[:, columns(h)] = key.astype(BF16)
            value = vg_part[h] + reaches[...] * nn(rows_of(KEY, h), back)
            o_v[:, columns(h)] = value.astype(BF16)

    for h in range(OWN_HEADS):
        norm(h)
    for h in range(OWN_HEADS - 2):
        partial(h)
    for j in range(len(BACK)):
        b_total(j)
    for h in range(OWN_HEADS - 2, OWN_HEADS):
        partial(h)
    for j in range(len(BACK)):
        b_carry(j)
    for j in range(len(BACK)):
        finish(j)

    def left(ref, stage):
        pltpu.make_async_copy(ref, ref, send_sem.at[stage]).wait()

    left(seg_line.at[0 : LINES - 1], 1)
    left(seg_all.at[0 : GROUP - 1], 3)
    left(sq_recv.at[0 : HEAD_PEERS - 1], 10)
    for j in range(len(AHEAD)):
        left(a[j].at[:, 0 : ROWS - BAND], 0)
        left(c[j].at[:, 0 : ROWS - BAND], 2)
        left(sf[j].at[0 : GROUP - 1], 4)
        left(zrf[j], 5)
        left(csf[j].at[0 : GROUP - 1], 6)
    for j in range(len(BACK)):
        left(sb[j].at[0 : GROUP - 1], 7)
        left(zrb[j], 8)
        left(csb[j].at[0 : GROUP - 1], 9)


def deliver(n_in, q_in, k_in, v_in, n_out, q_out, k_out, v_out, sem):
    copies = []
    for i, (src, dst) in enumerate(((n_in, n_out), (q_in, q_out), (k_in, k_out), (v_in, v_out))):
        copy = pltpu.make_async_copy(src, dst, sem.at[i])
        copy.start()
        copies.append(copy)
    for copy in copies:
        copy.wait()


def shards(queries, keys, values, normed_grad, gain, segment, plan):
    vm = pltpu.VMEM

    def per(chunks, shape):
        return [vm(shape(n), BF16) for n in chunks]

    parcels = per(AHEAD, lambda n: (3, ROWS, n * HEAD_DIM))
    square = vm((ROWS, ROWS), F32)
    square_b = vm((ROWS, ROWS), BF16)
    by_head = vm((OWN_HEADS, ROWS, HEAD_DIM), BF16)
    by_head_f = vm((OWN_HEADS, ROWS, HEAD_DIM), F32)

    def state_set(chunks):
        states = per(chunks, lambda n: (GROUP, n, PIECE, HEAD_DIM))
        return [
            states, states, per(chunks, lambda n: (n, PIECE, HEAD_DIM)),
            per(chunks, lambda n: (2, n, PIECE, HEAD_DIM)), states, states,
        ]

    out = vm((ROWS, OWN_HEADS * HEAD_DIM), BF16)
    inputs = (
        queries, keys, values, normed_grad,
        gain, segment.reshape(1, -1), plan.reshape(LINES * GROUP, ROWS),
    )
    results = pl.pallas_call(
        kernel,
        out_shape=(out, out, out, out),
        in_specs=[pl.BlockSpec(memory_space=pltpu.HBM)] * 7,
        out_specs=[pl.BlockSpec(memory_space=pltpu.VMEM)] * 4,
        scratch_shapes=[
            parcels, parcels, parcels, parcels, parcels, parcels,
            vm((ROWS, OWN_HEADS * HEAD_DIM), BF16), vm((OWN_HEADS * HEAD_DIM,), BF16),
            vm((OWN_HEADS, 1, HEAD_DIM), F32),
            vm((1, ROWS), jnp.int32), vm((LINES * GROUP, ROWS), jnp.int32),
            vm((LINES, 2, ROWS), F32), vm((GROUP, LINES, 2, ROWS), F32),
            square_b, square_b, square, square, square_b, square_b, square, square,
            *state_set(AHEAD), *state_set(BACK),
            by_head, by_head, by_head, vm((8, ROWS), F32), vm((HEAD_PEERS, 8, ROWS), F32),
            by_head_f, by_head_f,
            pltpu.SemaphoreType.DMA((len(PARCELS) + 4,)),
            pltpu.SemaphoreType.DMA((11,)),
            pltpu.SemaphoreType.DMA((2, len(PARCELS))),
            pltpu.SemaphoreType.DMA((6, max(len(AHEAD), len(BACK)))),
            pltpu.SemaphoreType.DMA((3,)),
        ],
        compiler_params=pltpu.CompilerParams(
            collective_id=0, has_side_effects=True, vmem_limit_bytes=40 << 20
        ),
    )(*(pltpu.with_memory_space_constraint(t, pltpu.HBM) for t in inputs))
    final = jax.ShapeDtypeStruct(queries.shape, BF16)
    return tuple(pl.pallas_call(
        deliver,
        out_shape=(final, final, final, final),
        in_specs=[pl.BlockSpec(memory_space=pltpu.VMEM)] * 4,
        out_specs=[pl.BlockSpec(memory_space=pltpu.HBM)] * 4,
        scratch_shapes=[pltpu.SemaphoreType.DMA((4,))],
    )(*(pltpu.with_memory_space_constraint(t, pltpu.VMEM) for t in results)))


def solution(mesh):
    both = P("ctx", "head")
    return jax.shard_map(
        shards,
        mesh=mesh,
        in_specs=(both, both, both, both, P("head"), P("ctx"), P()),
        out_specs=(both, both, both, both),
        check_vma=False,
    )
```

time: 72.5 us -> 68.7 us (0.948)
  Pallas kernels: 70.4 us -> 68 us
  local copies, waits for them, and re-layouts: 1.28 us -> 0 us
    pallas_call x1, Pallas kernels: 69.2 us -> 66.8 us  [shards(): pl.pallas_call(kernel, out_shape=(out, out, out, out), in_specs=[pl.Block...]
    reshape x1 -> x0, local copies, waits for them, and re-layouts: 1.28 us -> none  [shards(): gain.reshape(1, -1)]
where the time goes in v3:
time: 68.7 us; the launch traced here: 68.6 us
  Pallas kernels  68 us (99%)
    pallas_call x1, Pallas kernels, shards(): pl.pallas_call(kernel, out_shape=(out, out, out, out), in_specs=[pl.Block...  66.8 us

profile of v3, /device:TPU:1, one launch (start us, length us, event | category | flops | bytes accessed | tf_op | source)
XLA Modules:
  0.0 68.6 jit_solution(13232130556365219699)
XLA Ops:
  0.6 66.8 %shard_map.102 = (bf16[128,1536]{1,0:T(8,128)(2,1)S(1)}, bf16[128,1536]{1,0:T(8,128)(2,1)S(1)}, bf16[128,1536]{1,0:T(8,128)(2,1)S(1)}, bf16[128,1536]{1,0:T(8,128)(2,1)S(1)}) custom-call(bf16[128,1536]{1,0:T(8,128)(2,1)} %q_hbm.1, bf16[128,1536]{1,0:T(8,128)(2,1)} %k_hbm.1, bf16[128,1536]{1,0:T(8,128)(2,1)} %v_hbm.1, bf16[128,1536]{1,0:T(8,128)(2,1)} %ng_hbm.1, ...), custom_call_target="tpu_custom_call" | custom-call | tf_op jit(solution)/shard_map/pallas_call | solution.py:473
  67.4 1.2 %shard_map.103 = (bf16[128,1536]{1,0:T(8,128)(2,1)}, bf16[128,1536]{1,0:T(8,128)(2,1)}, bf16[128,1536]{1,0:T(8,128)(2,1)}, bf16[128,1536]{1,0:T(8,128)(2,1)}) custom-call(bf16[128,1536]{1,0:T(8,128)(2,1)S(1)} %get-tuple-element.8.n_in, bf16[128,1536]{1,0:T(8,128)(2,1)S(1)} %get-tuple-element.9.q_in, bf16[128,1536]{1,0:T(8,128)(2,1)S(1)} %get-tuple-element.10.k_in, ...), custom_call_target="tpu_custom_call" | custom-call | tf_op jit(solution)/shard_map/pallas_call | solution.py:499

commit v4 on v3

--- a/solution.py
+++ b/solution.py
@@ -11,9 +11,10 @@
 LINES = 8
 GROUP = 8
 OWN_HEADS = 12
-AHEAD = (4, 4, 3, 1)
+AHEAD = (4, 3, 3, 2)
 BACK = (2, 4, 4, 2)
 BAND = ROWS // LINES
+WINDOW = 2.0
 PIECE = HEAD_DIM // GROUP
 HEAD_PEERS = 4
 MESH = pl.DeviceIdType.MESH
@@ -38,25 +39,37 @@
 
 
 def timeline():
-    wire_z, late_z, wire_x, late_x, wire_line, late_line = 0.7, 4.0, 0.36, 3.5, 0.2, 3.3
-    events, second, clock = [], {}, 0.0
-    for p, (t, j) in enumerate(PARCELS):
+    wire_z, late_z, wire_x, late_x, wire_line, late_line = 0.7, 4.0, 0.36, 3.2, 0.26, 3.0
+    starts, clock = [], 0.0
+    for t, j in PARCELS:
+        starts.append(clock)
         clock += wire_z * AHEAD[j]
-        first = clock + late_z
-        events.append((first, "first_hop", p))
-        second[t, j] = first + late_x + wire_x * AHEAD[j]
-        events.append((second[t, j], "second_hop", p))
-    for j, heads in enumerate(AHEAD):
-        ready = second[VALUE, j] + 0.01
-        events.append((ready, "forward_state", j))
-        ready += late_x + (wire_x + 0.1) * heads
-        events.append((ready, "f_total", j))
-        clock = max(clock, ready) + wire_line * heads
-        ready = clock + late_line
-        events.append((ready, "f_carry", j))
-        ready = max(ready + late_x + wire_x * heads, second[QUERY, j] + 0.02)
+    totals = [99.0 + j for j in range(len(AHEAD))]
+    for _ in range(4):
+        queue = [(start - WINDOW, wire_z * AHEAD[j], ("p", p)) for p, ((t, j), start) in enumerate(zip(PARCELS, starts))]
+        queue += [(when, wire_line * AHEAD[j], ("r", j)) for j, when in enumerate(totals)]
+        clock, there = 0.0, {}
+        for issue, takes, what in sorted(queue):
+            clock = max(clock, issue) + takes
+            there[what] = clock
+        second = {
+            parcel: there["p", p] + late_z + 4.4 + 0.1 * AHEAD[parcel[1]]
+            for p, parcel in enumerate(PARCELS)
+        }
+        totals = [second[VALUE, j] + 0.02 + late_x + 0.3 * n for j, n in enumerate(AHEAD)]
+    events = []
+    for p, parcel in enumerate(PARCELS):
+        if starts[p] > WINDOW:
+            events.append((starts[p] - WINDOW, "depart", p))
+        events.append((there["p", p] + late_z, "first_hop", p))
+        events.append((second[parcel], "second_hop", p))
+    for j, n in enumerate(AHEAD):
+        carry = there["r", j] + late_line
+        events.append((second[VALUE, j] + 0.01, "forward_state", j))
+        events.append((totals[j], "f_total", j))
+        events.append((carry, "f_carry", j))
         events.append((second[QUERY, j] + 0.01, "weigh", j))
-        events.append((ready, "attend", j))
+        events.append((max(carry + late_x + wire_x * n, second[QUERY, j] + 0.02), "attend", j))
     return [event[1:] for event in sorted(events)]
 
 
@@ -166,13 +179,15 @@
 
     pl.semaphore_wait(barrier, LINES - 1 + GROUP - 1 + HEAD_PEERS - 1)
 
+    steps = timeline()
     for dz in Z_ORDER:
         send(seg_line.at[z], seg_line.at[z], 1, small_sem.at[0], ctx_of(z_peer(dz), g), y)
     depart(0)
     for p, (t, j) in enumerate(PARCELS):
         if p > 0:
             sort(p)
-            depart(p)
+            if ("depart", p) not in steps:
+                depart(p)
 
     seg_lanes = jnp.broadcast_to(seg_f, (ROWS, ROWS))
     seg_rows = seg_lanes.T
@@ -354,10 +369,10 @@
         sums.append((squares, inner))
 
     work = dict(
-        first_hop=first_hop, second_hop=second_hop, forward_state=forward_state,
+        depart=depart, first_hop=first_hop, second_hop=second_hop, forward_state=forward_state,
         f_total=f_total, f_carry=f_carry, weigh=weigh, attend=attend,
     )
-    for name, n in timeline():
+    for name, n in steps:
         work[name](n)
 
     squares = sum(one for one, _ in sums)

time: 68.7 us -> 66.5 us (0.968)
  Pallas kernels: 68 us -> 65.7 us
    pallas_call x1, Pallas kernels: 66.8 us -> 64.5 us  [shards(): pl.pallas_call(kernel, out_shape=(out, out, out, out), in_specs=[pl.Block...]
where the time goes in v4:
time: 66.5 us; the launch traced here: 66.4 us
  Pallas kernels  65.7 us (99%)
    pallas_call x1, Pallas kernels, shards(): pl.pallas_call(kernel, out_shape=(out, out, out, out), in_specs=[pl.Block...  64.5 us

profile of v4, /device:TPU:1, one launch (start us, length us, event | category | flops | bytes accessed | tf_op | source)
XLA Modules:
  0.0 66.4 jit_solution(12356597432444198780)
XLA Ops:
  0.6 64.5 %shard_map.102 = (bf16[128,1536]{1,0:T(8,128)(2,1)S(1)}, bf16[128,1536]{1,0:T(8,128)(2,1)S(1)}, bf16[128,1536]{1,0:T(8,128)(2,1)S(1)}, bf16[128,1536]{1,0:T(8,128)(2,1)S(1)}) custom-call(bf16[128,1536]{1,0:T(8,128)(2,1)} %q_hbm.1, bf16[128,1536]{1,0:T(8,128)(2,1)} %k_hbm.1, bf16[128,1536]{1,0:T(8,128)(2,1)} %v_hbm.1, bf16[128,1536]{1,0:T(8,128)(2,1)} %ng_hbm.1, ...), custom_call_target="tpu_custom_call" | custom-call | tf_op jit(solution)/shard_map/pallas_call | solution.py:488
  65.2 1.2 %shard_map.103 = (bf16[128,1536]{1,0:T(8,128)(2,1)}, bf16[128,1536]{1,0:T(8,128)(2,1)}, bf16[128,1536]{1,0:T(8,128)(2,1)}, bf16[128,1536]{1,0:T(8,128)(2,1)}) custom-call(bf16[128,1536]{1,0:T(8,128)(2,1)S(1)} %get-tuple-element.8.n_in, bf16[128,1536]{1,0:T(8,128)(2,1)S(1)} %get-tuple-element.9.q_in, bf16[128,1536]{1,0:T(8,128)(2,1)S(1)} %get-tuple-element.10.k_in, ...), custom_call_target="tpu_custom_call" | custom-call | tf_op jit(solution)/shard_map/pallas_call | solution.py:514
